TPU v7x, 256 devices: a whole 4x4x8 slice. The times are simulated.
256 devices in a mesh: ent: 64 (over x, z, core), rel: 4 (over y).
Axes of the slice: x: 4, y: 4, z: 8, core: 2. Of those that a mesh axis runs over, the one named last changes fastest.
Arguments:
- state_zero: bfloat16 [65536, 256], P('ent'), may hold values from -6 to 6
- state_one: bfloat16 [65536, 256], P('ent'), may hold values from -6 to 6
- aggregate_one: bfloat16 [65536, 256], P('ent'), may hold values from -6 to 6
- aggregate_two: bfloat16 [65536, 256], P('ent'), may hold values from -6 to 6
- cotangent: bfloat16 [65536, 256], P('ent'), may hold values from -6 to 6
- relation_table: bfloat16 [1312, 256], P('rel'), may hold values from -6 to 6
- update_in: bfloat16 [2, 64, 256], replicated, may hold values from -0.75 to 0.75
- update_bias: float32 [2, 256], replicated, may hold values from -3 to 3
- update_out: bfloat16 [2, 256, 32], replicated, may hold values from -0.375 to 0.375
- frontier_tiles: int32 [2, 128], P(None, 'ent'), may hold values from 0 to 7, as said below
- frontier_count: int32 [2, 64], P(None, 'ent'), may hold values from 1 to 2, as said below
- edge_source: int32 [262144], P(('ent', 'rel')), may hold values from 0 to 1023
- edge_relation: int32 [262144], P(('ent', 'rel')), may hold values from 0 to 327
- edge_target: int32 [262144], P(('ent', 'rel')), may hold values from 0 to 1023
- edge_owner: int32 [262144, 1], P(('ent', 'rel')), may hold values from 0 to 63; in each aligned block of 1024 rows (0 to 1023, 1024 to 2047, ...) at most 24 rows name the same one
Outputs:
- grad_state_zero: bfloat16 [65536, 256], P(('ent', 'rel'))
- grad_relation: float32 [1312, 256], P('rel')
- grad_update_in: float32 [2, 64, 256], replicated
- grad_update_bias: float32 [2, 256], replicated
- grad_update_out: float32 [2, 256, 32], replicated
Inputs may be any that keep to these rules, and one draw needn't show every extreme that they name: `frontier_tiles`: within one owner's 2 slots of a hop the tile numbers are distinct, padded slots included. The first frontier_count entries of an owner's list are its live tiles; in each hop some owner has all 2 live. `edge_owner`: among the 1024 edges of one device at most 24 name the same owner, and in some device some owner is named by exactly 24.
All inputs are finite; a program needn't handle non-finite values.
Results may differ from a plain program's by a relative error of at most 0.009.
Values may be sent and summed in bfloat16 or wider, within the bound.
No kernel may reach another device: no remote copies, remote signals or barrier semaphores. Data moves between devices by JAX's collectives and lax.ppermute only.
A program may use at most 64 MiB of HBM per device.

v0:
```python
import math
import jax
import jax.numpy as jnp
from jax import lax
from jax.sharding import PartitionSpec as P

QUERIES = 8
DIM = 32
TILE = 128


def frontier_rows(tile_ids, live_count, tile_total):
    slot_valid = jnp.arange(tile_ids.shape[0], dtype=jnp.int32) < live_count
    tile_range = jnp.arange(tile_total, dtype=jnp.int32)
    matched = (tile_ids[None, :] == tile_range[:, None]) & slot_valid[None, :]
    return jnp.repeat(jnp.any(matched, axis=1).astype(jnp.float32), TILE)


def exact_pick_sum(selector, values, contract_dim):
    high_part = values.astype(jnp.bfloat16)
    low_part = (values - high_part.astype(jnp.float32)).astype(jnp.bfloat16)
    numbers = (((contract_dim,), (0,)), ((), ()))
    first = lax.dot_general(selector, high_part, numbers, preferred_element_type=jnp.float32)
    second = lax.dot_general(selector, low_part, numbers, preferred_element_type=jnp.float32)
    return first + second


def update_backward(aggregate, state, upstream, update_in, update_bias, update_out):
    row_count = aggregate.shape[0]
    inputs = jnp.concatenate(
        [aggregate.reshape(row_count, QUERIES, DIM), state.reshape(row_count, QUERIES, DIM)], axis=2
    )
    pre_act = (
        jnp.einsum("nqd,de->nqe", inputs, update_in, preferred_element_type=jnp.float32)
        + update_bias
    )
    gate_value = jax.nn.sigmoid(pre_act)
    activated = (pre_act * gate_value).astype(jnp.bfloat16)
    slope = gate_value * (1.0 + pre_act * (1.0 - gate_value))
    upstream_low = upstream.astype(jnp.bfloat16).reshape(row_count, QUERIES, DIM)
    grad_act = jnp.einsum(
        "nqd,ed->nqe", upstream_low, update_out, preferred_element_type=jnp.float32
    )
    grad_pre = grad_act * slope
    grad_pre_low = grad_pre.astype(jnp.bfloat16)
    grad_out = jnp.einsum(
        "nqe,nqd->ed", activated, upstream_low, preferred_element_type=jnp.float32
    )
    grad_bias = jnp.sum(grad_pre, axis=(0, 1))
    grad_in = jnp.einsum("nqd,nqe->de", inputs, grad_pre_low, preferred_element_type=jnp.float32)
    grad_inputs = jnp.einsum(
        "nqe,de->nqd", grad_pre_low, update_in, preferred_element_type=jnp.float32
    )
    grad_agg = grad_inputs[:, :, :DIM].reshape(row_count, QUERIES * DIM).astype(jnp.bfloat16)
    grad_state = grad_inputs[:, :, DIM:].reshape(row_count, QUERIES * DIM)
    return (grad_agg, grad_state, grad_in, grad_bias, grad_out)


def mlp_blocks(aggregate, state, upstream, update_in, update_bias, update_out):
    row_count = aggregate.shape[0]
    feature_width = aggregate.shape[1]
    block_rows = math.gcd(row_count, 512)
    block_count = row_count // block_rows

    def step(carry, pieces):
        grad_agg, grad_state, grad_in, grad_bias, grad_out = update_backward(
            pieces[0], pieces[1], pieces[2], update_in, update_bias, update_out
        )
        return (
            (carry[0] + grad_in, carry[1] + grad_bias, carry[2] + grad_out),
            (grad_agg, grad_state),
        )

    initial = (
        jnp.zeros(update_in.shape, jnp.float32),
        jnp.zeros(update_bias.shape, jnp.float32),
        jnp.zeros(update_out.shape, jnp.float32),
    )
    stacked = tuple(
        (
            source_array.reshape(block_count, block_rows, feature_width)
            for source_array in (aggregate, state, upstream)
        )
    )
    sums, (grad_agg, grad_state) = lax.scan(step, initial, stacked)
    return (
        grad_agg.reshape(row_count, feature_width),
        grad_state.reshape(row_count, feature_width),
        sums,
    )


def shards(
    state_zero,
    state_one,
    aggregate_one,
    aggregate_two,
    cotangent,
    relation_table,
    update_in,
    update_bias,
    update_out,
    frontier_tiles,
    frontier_count,
    edge_source,
    edge_relation,
    edge_target,
    edge_owner,
):
    block_rows = state_zero.shape[0]
    feature_width = state_zero.shape[1]
    group_size = lax.axis_size("rel")
    peer_count = lax.axis_size("ent")
    quarter = block_rows // group_size
    quarter_start = lax.axis_index("rel") * quarter
    edge_count = edge_source.shape[0]
    capacity = 3 * edge_count // (2 * peer_count)
    tile_total = block_rows // TILE
    group_width = relation_table.shape[0]
    edge_peer = edge_owner[:, 0]
    onehot = (edge_peer[:, None] == jnp.arange(peer_count, dtype=jnp.int32)[None, :]).astype(
        jnp.int32
    )
    earlier = jnp.sum((jnp.cumsum(onehot, axis=0) - onehot) * onehot, axis=1)
    edge_slot = edge_peer * capacity + earlier
    request = jnp.zeros((peer_count * capacity,), jnp.int32).at[edge_slot].set(edge_target)
    asked = lax.all_to_all(
        request.reshape(peer_count, capacity), "ent", split_axis=0, concat_axis=0, tiled=True
    )
    source_select = (
        jnp.arange(block_rows, dtype=jnp.int32)[:, None] == edge_source[None, :]
    ).astype(jnp.bfloat16)
    relation_select = (
        edge_relation[:, None] == jnp.arange(group_width, dtype=jnp.int32)[None, :]
    ).astype(jnp.bfloat16)
    edge_table = jnp.dot(relation_select, relation_table, preferred_element_type=jnp.float32)
    upstream = cotangent.astype(jnp.float32)
    relation_grad = jnp.zeros((group_width, feature_width), jnp.float32)
    layer_sums = [None, None]
    for aggregate, state, layer in ((aggregate_two, state_one, 1), (aggregate_one, state_zero, 0)):
        grad_agg, grad_state, sums = mlp_blocks(
            aggregate, state, upstream, update_in[layer], update_bias[layer], update_out[layer]
        )
        picked = grad_agg[asked]
        answered = lax.all_to_all(picked, "ent", split_axis=0, concat_axis=0, tiled=True)
        served = answered.reshape(peer_count * capacity, feature_width)[edge_slot]
        tile_ids = frontier_tiles[layer]
        row_mask = frontier_rows(tile_ids, frontier_count[layer, 0], tile_total)
        weighted = served.astype(jnp.float32) * row_mask[edge_source][:, None]
        contrib = exact_pick_sum(source_select, weighted * edge_table, 1)
        relation_grad = relation_grad + exact_pick_sum(
            relation_select, weighted * state[edge_source].astype(jnp.float32), 0
        )
        source_grad = lax.psum(contrib.astype(jnp.bfloat16), "rel").astype(jnp.float32)
        upstream = upstream + grad_state + source_grad
        layer_sums[layer] = sums
    stacked_in = jnp.stack([layer_sums[0][0], layer_sums[1][0]])
    stacked_bias = jnp.stack([layer_sums[0][1], layer_sums[1][1]])
    stacked_out = jnp.stack([layer_sums[0][2], layer_sums[1][2]])
    grad_in_all, grad_bias_all, grad_out_all, relation_total = lax.psum(
        (stacked_in, stacked_bias, stacked_out, relation_grad), "ent"
    )
    scale_weights = 1.0 / math.sqrt(block_rows * peer_count * QUERIES)
    scale_relations = math.sqrt(group_width * group_size / (edge_count * peer_count * group_size))
    return (
        lax.dynamic_slice_in_dim(upstream, quarter_start, quarter, 0).astype(jnp.bfloat16),
        relation_total * scale_relations,
        grad_in_all * scale_weights,
        grad_bias_all * scale_weights,
        grad_out_all * scale_weights,
    )


def solution(mesh):
    in_specs = (
        P("ent", None),
        P("ent", None),
        P("ent", None),
        P("ent", None),
        P("ent", None),
        P("rel", None),
        P(),
        P(),
        P(),
        P(None, "ent"),
        P(None, "ent"),
        P(("ent", "rel")),
        P(("ent", "rel")),
        P(("ent", "rel")),
        P(("ent", "rel"), None),
    )
    out_specs = (P(("ent", "rel"), None), P("rel", None), P(), P(), P())
    return jax.shard_map(shards, mesh=mesh, in_specs=in_specs, out_specs=out_specs, check_vma=False)
```

profile of v0, /device:TPU:2, one launch (start us, length us, event | category | flops | bytes accessed | tf_op | source)
XLA Modules:
  0.0 626.9 jit_solution(3884639619966283850)
XLA Ops:
  7.9 18.0 %reduce-window.6 = s32[64,8,128]{2,1,0:T(8,128)S(1)} reduce-window(s32[64,8,128]{2,1,0:T(8,128)S(1)} %fusion.77, s32[]{:T(128)} %constant.31.clone.1), window={size=1x1x128 pad=0_0x0_0x127_0}, to_apply=%region_3.4 | reduce-window | flops 8323072 | bytes 524292 | tf_op jit(solution)/shard_map/reduce-window
  28.0 4.5 scatter_custom_fusion
  33.1 12.0 %all-to-all-start = ((s32[64,1,24]{2,1,0:T(1,128)}), s32[64,1,24]{2,1,0:T(1,128)S(1)}, u32[]{:S(2)}, u32[]{:S(2)}) async-start(s32[64,1,24]{2,1,0:T(1,128)} %bitcast.13), calls=%async_computation | async-start | bytes 65536 | tf_op jit(solution)/shard_map/all_to_all | solution.py:127
  49.7 36.1 %while.38 = (s32[]{:T(128)}, f32[64,256]{1,0:T(8,128)S(1)}, f32[256]{0:T(256)S(1)}, f32[256,32]{0,1:T(8,128)S(1)}, bf16[2,512,256]{2,1,0:T(8,128)(2,1)S(1)}, /*i...) while((s32[]{:T(128)}, f32[64,256]{1,0:T(8,128)S(1)}, ...), condition=%wide.region_2.3_spmd.clone, body=%wide.region_0.2_spmd.clone.sunk | while | flops 556843264 | bytes 33839300 | solution.py:85
  55.6 4.0 fusion.123
  60.2 3.5 fusion.125
  70.1 2.7 fusion.122
  73.7 4.0 fusion.123
  78.3 3.5 fusion.125
  86.0 5.4 gather_fusion
  91.4 10.5 %all-to-all-start.1 = ((bf16[64,24,256]{2,1,0:T(8,128)(2,1)}), bf16[64,24,256]{2,1,0:T(8,128)(2,1)S(1)}, u32[]{:S(2)}, u32[]{:S(2)}) async-start(bf16[64,24,256]{2,1,0:T(8,128)(2,1)} %bitcast.15), calls=%async_computation.1 | async-start | bytes 1572864 | tf_op jit(solution)/shard_map/all_to_all | solution.py:145
  104.7 4.5 gather_fusion.2
  109.8 13.9 %all-to-all-done.1 = bf16[64,24,256]{2,1,0:T(8,128)(2,1)S(1)} async-done(((bf16[64,24,256]{2,1,0:T(8,128)(2,1)}), bf16[64,24,256]{2,1,0:T(8,128)(2,1)S(1)}, u32[]{:S(2)}, u32[]{:S(2)}) %all-to-all-start.1) | async-done | bytes 786464 | tf_op jit(solution)/shard_map/all_to_all | solution.py:145
  123.7 3.9 gather_fusion.1
  130.5 46.5 %all-reduce.5.cloned.1.call-done = bf16[1024,256]{1,0:T(8,128)(2,1)} async-done(((bf16[1024,256]{1,0:T(8,128)(2,1)}), bf16[1024,256]{1,0:T(8,128)(2,1)}) %all-reduce.5.cloned.1.call-update) | async-done | bytes 524304 | tf_op jit(solution)/shard_map/psum | solution.py:154
  180.8 35.8 %while.39 = (s32[]{:T(128)}, f32[64,256]{1,0:T(8,128)S(1)}, f32[256]{0:T(256)S(1)}, f32[256,32]{0,1:T(8,128)S(1)}, bf16[2,512,256]{2,1,0:T(8,128)(2,1)S(1)}, /*i...) while((s32[]{:T(128)}, f32[64,256]{1,0:T(8,128)S(1)}, ...), condition=%wide.region_11.12_spmd.clone, body=%wide.region_9.11_spmd.clone.sunk | while | flops 556843264 | bytes 33839300 | solution.py:85
  183.2 2.7 fusion.133
  186.7 4.0 fusion.134
  191.2 3.4 fusion.136
  204.6 4.0 fusion.134
  209.1 3.4 fusion.136
  216.6 5.4 gather_fusion.3
  222.0 10.5 %all-to-all-start.2 = ((bf16[64,24,256]{2,1,0:T(8,128)(2,1)}), bf16[64,24,256]{2,1,0:T(8,128)(2,1)S(1)}, u32[]{:S(2)}, u32[]{:S(2)}) async-start(bf16[64,24,256]{2,1,0:T(8,128)(2,1)} %bitcast.27), calls=%async_computation.2 | async-start | bytes 1572864 | tf_op jit(solution)/shard_map/all_to_all | solution.py:145
  232.8 5.7 gather_fusion.7
  238.5 4.6 gather_fusion.6
  243.3 4.5 gather_fusion.5
  249.5 107.1 %psum.46 = f32[2,256]{1,0:T(2,128)S(1)} all-reduce(f32[2,256]{1,0:T(2,128)S(1)} %pad_maximum_fusion.8), channel_id=1, replica_groups=mesh['ent'=64,'rel'=4] {'ent'}, use_global_device_ids=true, to_apply=%region_16.17 | all-reduce | flops 512 | bytes 4096 | tf_op jit(solution)/shard_map/psum | solution.py:160
  358.4 4.9 gather_fusion.4
  363.4 3.1 fusion.28
  371.4 3.0 fusion.43
  374.4 196.0 %all-reduce.9.cloned.1.call-done = (f32[328,256]{1,0:T(8,128)}, f32[2,64,256]{2,1,0:T(8,128)}, f32[2,256,32]{1,2,0:T(8,128)}) async-done(((f32[328,256]{1,0:T(8,128)}, f32[2,64,256]{2,1,0:T(8,128)}, f32[2,256,32]{1,2,0:T(8,128)}), (f32[328,256]{1,0:T(8,128)}, f32[2,64,256]{2,1,0:T(8,128)}, f32[2,256,32]{1,2,0:T(8,128)})) %all-reduce.9.cloned.1.call-update) | async-done | bytes 532496 | tf_op jit(solution)/shard_map/psum | solution.py:160
  575.1 43.5 %all-reduce.7.cloned.1.call-done = bf16[1024,256]{1,0:T(8,128)(2,1)} async-done(((bf16[1024,256]{1,0:T(8,128)(2,1)}), bf16[1024,256]{1,0:T(8,128)(2,1)}) %all-reduce.7.cloned.1.call-update) | async-done | bytes 524304 | tf_op jit(solution)/shard_map/psum | solution.py:154
  (170 shorter events, 69.4 us)
Async XLA Ops:
  7.2 102.1 %copy-start = (bf16[328,256]{1,0:T(8,128)(2,1)S(1)}, bf16[328,256]{1,0:T(8,128)(2,1)}, u32[]{:S(2)}) copy-start(bf16[328,256]{1,0:T(8,128)(2,1)} %param.24) | copy-start | bytes 503812
  33.1 52.7 %all-to-all-start = ((s32[64,1,24]{2,1,0:T(1,128)}), s32[64,1,24]{2,1,0:T(1,128)S(1)}, u32[]{:S(2)}, u32[]{:S(2)}) async-start(s32[64,1,24]{2,1,0:T(1,128)} %bitcast.13), calls=%async_computation | async-start | bytes 65536 | tf_op jit(solution)/shard_map/all_to_all | solution.py:127
  64.4 1.0 copy-start.1
  82.5 1.0 copy-start.1
  85.9 5.5 copy-start.11
  86.0 16.1 %copy-start.19 = (s32[2,1]{0,1:T(1,128)S(1)}, s32[2,1]{0,1:T(1,128)}, u32[]{:S(2)}) copy-start(s32[2,1]{0,1:T(1,128)} %param.29) | copy-start | bytes 28
  86.0 18.0 %copy-start.20 = (s32[2,2]{1,0:T(2,128)S(1)}, s32[2,2]{1,0:T(2,128)}, u32[]{:S(2)}) copy-start(s32[2,2]{1,0:T(2,128)} %param.28) | copy-start | bytes 52
  86.0 18.7 %copy-start.15 = (s32[1024]{0:T(1024)S(1)}, s32[1024]{0:T(1024)}, u32[]{:S(2)}) copy-start(s32[1024]{0:T(1024)} %param.30) | copy-start | bytes 12292
  91.4 17.9 %copy-start.13 = (s32[1024]{0:T(1024)S(1)}, s32[1024]{0:T(1024)}, u32[]{:S(2)}) copy-start(s32[1024]{0:T(1024)} %param.31) | copy-start | bytes 12292
  91.4 32.3 %all-to-all-start.1 = ((bf16[64,24,256]{2,1,0:T(8,128)(2,1)}), bf16[64,24,256]{2,1,0:T(8,128)(2,1)S(1)}, u32[]{:S(2)}, u32[]{:S(2)}) async-start(bf16[64,24,256]{2,1,0:T(8,128)(2,1)} %bitcast.15), calls=%async_computation.1 | async-start | bytes 1572864 | tf_op jit(solution)/shard_map/all_to_all | solution.py:145
  101.9 75.2 %all-reduce.5.cloned.1.call-start = ((), (), s32[]{:S(2)}) async-start(), calls=%async_computation.3 | async-start | bytes 1048576 | tf_op jit(solution)/shard_map/psum | solution.py:154
  109.2 19.4 %copy-start.17 = (f32[1024]{0:T(1024)}, f32[1024]{0:T(1024)S(1)}, u32[]{:S(2)}) copy-start(f32[1024]{0:T(1024)S(1)} %gather_fusion.2) | copy-start | bytes 12292
  109.8 18.9 %copy-start.5 = (f32[1024,256]{1,0:T(8,128)}, f32[1024,256]{1,0:T(8,128)S(1)}, u32[]{:S(2)}) copy-start(f32[1024,256]{1,0:T(8,128)S(1)} %fusion.40) | copy-start | bytes 3145732
  127.7 2.8 copy-start.7
  127.7 49.4 %copy-start.4 = (f32[2,512,256]{2,1,0:T(8,128)S(1)}, f32[2,512,256]{2,1,0:T(8,128)}, u32[]{:S(2)}) copy-start(f32[2,512,256]{2,1,0:T(8,128)} %get-tuple-element.137) | copy-start | bytes 3145732
  178.5 1.2 copy-start.3
  195.4 1.0 copy-start.2
  213.3 1.0 copy-start.2
  222.0 136.4 %all-to-all-start.2 = ((bf16[64,24,256]{2,1,0:T(8,128)(2,1)}), bf16[64,24,256]{2,1,0:T(8,128)(2,1)S(1)}, u32[]{:S(2)}, u32[]{:S(2)}) async-start(bf16[64,24,256]{2,1,0:T(8,128)(2,1)} %bitcast.27), calls=%async_computation.2 | async-start | bytes 1572864 | tf_op jit(solution)/shard_map/all_to_all | solution.py:145
  232.5 337.8 %all-reduce.9.cloned.1.call-start = ((), (), s32[]{:S(2)}) async-start(), calls=%async_computation.5 | async-start | bytes 1064960 | tf_op jit(solution)/shard_map/psum | solution.py:160
  232.8 10.4 %copy-start.21 = (pred[8]{0:T(512)(128)(4,1)S(1)}, pred[8]{0:T(512)(128)(4,1)}, u32[]{:S(2)}) copy-start(pred[8]{0:T(512)(128)(4,1)} %get-tuple-element.390) | copy-start | bytes 28
  238.5 9.3 %copy-start.8 = (bf16[1024,256]{1,0:T(8,128)(2,1)S(1)}, bf16[1024,256]{1,0:T(8,128)(2,1)}, u32[]{:S(2)}) copy-start(bf16[1024,256]{1,0:T(8,128)(2,1)} %copy-done.7) | copy-start | bytes 1572868
  238.5 9.3 %copy-start.14 = (s32[1024]{0:T(1024)S(1)}, s32[1024]{0:T(1024)}, u32[]{:S(2)}) copy-start(s32[1024]{0:T(1024)} %param.31) | copy-start | bytes 12292
  238.5 9.3 %copy-start.18 = (f32[1024]{0:T(1024)S(1)}, f32[1024]{0:T(1024)}, u32[]{:S(2)}) copy-start(f32[1024]{0:T(1024)} %copy-done.17) | copy-start | bytes 12292
  243.1 113.4 %copy-start.12 = (f32[256,32]{0,1:T(8,128)S(1)}, f32[256,32]{0,1:T(8,128)}, u32[]{:S(2)}) copy-start(f32[256,32]{0,1:T(8,128)} %copy-done.11) | copy-start | bytes 98308
  247.8 115.6 %copy-start.6 = (f32[1024,256]{1,0:T(8,128)S(1)}, f32[1024,256]{1,0:T(8,128)}, u32[]{:S(2)}) copy-start(f32[1024,256]{1,0:T(8,128)} %copy-done.5) | copy-start | bytes 3145732
  247.8 115.6 %copy-start.16 = (s32[1024]{0:T(1024)S(1)}, s32[1024]{0:T(1024)}, u32[]{:S(2)}) copy-start(s32[1024]{0:T(1024)} %param.30) | copy-start | bytes 12292
  363.4 5.3 copy-start.9
  363.4 5.3 copy-start.10
  363.4 6.2 copy-start.22
  371.3 247.3 %all-reduce.7.cloned.1.call-start = ((), (), s32[]{:S(2)}) async-start(), calls=%async_computation.4 | async-start | bytes 1048576 | tf_op jit(solution)/shard_map/psum | solution.py:154
Sparse Core Ops, SparseCore 0:
  130.6 46.4 all-reduce.4
  371.4 198.9 all-reduce.8
  572.7 45.8 all-reduce.6
where the time goes:
time: 628 us; the launch traced here: 627 us
  waiting for transfers between devices  300 us (48%)
  blocking collectives  107 us (17%)
  local copies, waits for them, and re-layouts  77.1 us (12%)
  matrix products  61.4 us (10%)
  starting transfers between devices  33.5 us (5%)
  other arithmetic  33.2 us (5%)
  between operations  14.3 us (2%)
    psum x1, waiting for transfers between devices, shards(): lax.psum((stacked_in, stacked_bias, stacked_out, relation_grad), 'ent')  196 us
    psum x1, blocking collectives, shards(): lax.psum((stacked_in, stacked_bias, stacked_out, relation_grad), 'ent')  107 us
    psum x2, waiting for transfers between devices, shards(): lax.psum(contrib.astype(jnp.bfloat16), 'rel').astype(jnp.float32)  90 us
    all_to_all x2, starting transfers between devices, shards(): lax.all_to_all(picked, 'ent', split_axis=0, concat_axis=0, tiled=True)  21 us
    another operation x3, other arithmetic  18.2 us
    dot_general x4, matrix products, update_backward(): jnp.einsum('nqd,ed->nqe', upstream_low, update_out, preferred_element_typ...  16 us
    all_to_all x2, waiting for transfers between devices, shards(): lax.all_to_all(picked, 'ent', split_axis=0, concat_axis=0, tiled=True)  13.9 us
    dot_general x4, matrix products, update_backward(): jnp.einsum('nqe,nqd->ed', activated, upstream_low, preferred_element_type...  13.9 us
  transfers between devices with their start and end apart: 6, of which 4 were waited for; matrix products, arithmetic and copies ran while one was open for 12% of the time, Pallas kernels for 0%

commit v1 on v0

--- a/solution.py
+++ b/solution.py
@@ -7,6 +7,11 @@
 QUERIES = 8
 DIM = 32
 TILE = 128
+
+
+def add_all(shard, mesh_axis):
+    pieces = lax.all_gather(shard, mesh_axis)
+    return jnp.sum(pieces, axis=0)
 
 
 def frontier_rows(tile_ids, live_count, tile_total):
@@ -151,7 +156,7 @@
         relation_grad = relation_grad + exact_pick_sum(
             relation_select, weighted * state[edge_source].astype(jnp.float32), 0
         )
-        source_grad = lax.psum(contrib.astype(jnp.bfloat16), "rel").astype(jnp.float32)
+        source_grad = add_all(contrib.astype(jnp.bfloat16), "rel").astype(jnp.float32)
         upstream = upstream + grad_state + source_grad
         layer_sums[layer] = sums
     stacked_in = jnp.stack([layer_sums[0][0], layer_sums[1][0]])

time: 628 us -> 481 us (0.77)
  waiting for transfers between devices: 300 us -> 149 us
    psum x1, waiting for transfers between devices: 196 us -> 71.5 us  [shards(): lax.psum((stacked_in, stacked_bias, stacked_out, relation_grad), 'ent')]
    psum x2 -> x0, waiting for transfers between devices: 90 us -> none  [shards(): lax.psum(contrib.astype(jnp.bfloat16), 'rel').astype(jnp.float32)]
    all_gather x0 -> x2, waiting for transfers between devices: none -> 59.8 us  [add_all(): pieces = lax.all_gather(shard, mesh_axis)]
  transfers between devices with their start and end apart: 6 -> 6, of which waited for: 4 -> 5; matrix products, arithmetic and copies ran while one was open for 12% -> 15% of each run, Pallas kernels for 0% -> 0%
where the time goes in v1:
time: 481 us; the launch traced here: 479 us
  waiting for transfers between devices  149 us (31%)
  blocking collectives  106 us (22%)
  local copies, waits for them, and re-layouts  77.1 us (16%)
  matrix products  61.5 us (13%)
  other arithmetic  37.4 us (8%)
  starting transfers between devices  33.6 us (7%)
  between operations  14.3 us (3%)
    psum x1, blocking collectives, shards(): lax.psum((stacked_in, stacked_bias, stacked_out, relation_grad), 'ent')  106 us
    psum x1, waiting for transfers between devices, shards(): lax.psum((stacked_in, stacked_bias, stacked_out, relation_grad), 'ent')  71.5 us
    all_gather x2, waiting for transfers between devices, add_all(): pieces = lax.all_gather(shard, mesh_axis)  59.8 us
    all_to_all x2, starting transfers between devices, shards(): lax.all_to_all(picked, 'ent', split_axis=0, concat_axis=0, tiled=True)  21 us
    another operation x3, other arithmetic  18.2 us
    all_to_all x2, waiting for transfers between devices, shards(): lax.all_to_all(picked, 'ent', split_axis=0, concat_axis=0, tiled=True)  17.6 us
    dot_general x4, matrix products, update_backward(): jnp.einsum('nqd,ed->nqe', upstream_low, update_out, preferred_element_typ...  16 us
    dot_general x4, matrix products, update_backward(): jnp.einsum('nqe,nqd->ed', activated, upstream_low, preferred_element_type...  13.9 us
  transfers between devices with their start and end apart: 6, of which 5 were waited for; matrix products, arithmetic and copies ran while one was open for 15% of the time, Pallas kernels for 0%

profile of v1, /device:TPU:2, one launch (start us, length us, event | category | flops | bytes accessed | tf_op | source)
XLA Modules:
  0.0 479.0 jit_solution(56745293016583004)
XLA Ops:
  7.9 18.0 %reduce-window.6 = s32[64,8,128]{2,1,0:T(8,128)S(1)} reduce-window(s32[64,8,128]{2,1,0:T(8,128)S(1)} %fusion.77, s32[]{:T(128)} %constant.27.clone.1), window={size=1x1x128 pad=0_0x0_0x127_0}, to_apply=%region_3.4 | reduce-window | flops 8323072 | bytes 524292 | tf_op jit(solution)/shard_map/reduce-window
  28.0 4.5 scatter_custom_fusion
  33.1 12.0 %all-to-all-start = ((s32[64,1,24]{2,1,0:T(1,128)}), s32[64,1,24]{2,1,0:T(1,128)S(1)}, u32[]{:S(2)}, u32[]{:S(2)}) async-start(s32[64,1,24]{2,1,0:T(1,128)} %bitcast.13), calls=%async_computation | async-start | bytes 65536 | tf_op jit(solution)/shard_map/all_to_all | solution.py:132
  49.7 36.1 %while.38 = (s32[]{:T(128)}, f32[64,256]{1,0:T(8,128)S(1)}, f32[256]{0:T(256)S(1)}, f32[256,32]{0,1:T(8,128)S(1)}, bf16[2,512,256]{2,1,0:T(8,128)(2,1)S(1)}, /*i...) while((s32[]{:T(128)}, f32[64,256]{1,0:T(8,128)S(1)}, ...), condition=%wide.region_2.3_spmd.clone, body=%wide.region_0.2_spmd.clone.sunk | while | flops 556843264 | bytes 33839300 | solution.py:90
  55.6 4.0 fusion.123
  60.2 3.5 fusion.125
  70.1 2.7 fusion.122
  73.7 4.0 fusion.123
  78.3 3.5 fusion.125
  86.0 5.4 %gather_fusion = bf16[1536,256]{1,0:T(8,128)(2,1)} fusion(bf16[1024,256]{1,0:T(8,128)(2,1)S(1)} %bitcast.188, s32[2048]{0:T(1024)S(1)} %pad_clamp_fusion), kind=kCustom, calls=%fused_computation | custom fusion | bytes 1579008 | tf_op jit(solution)/shard_map/gather | solution.py:149
  91.4 10.5 %all-to-all-start.1 = ((bf16[64,24,256]{2,1,0:T(8,128)(2,1)}), bf16[64,24,256]{2,1,0:T(8,128)(2,1)S(1)}, u32[]{:S(2)}, u32[]{:S(2)}) async-start(bf16[64,24,256]{2,1,0:T(8,128)(2,1)} %bitcast.15), calls=%async_computation.1 | async-start | bytes 1572864 | tf_op jit(solution)/shard_map/all_to_all | solution.py:150
  104.7 4.5 gather_fusion.2
  109.8 13.9 %all-to-all-done.1 = bf16[64,24,256]{2,1,0:T(8,128)(2,1)S(1)} async-done(((bf16[64,24,256]{2,1,0:T(8,128)(2,1)}), bf16[64,24,256]{2,1,0:T(8,128)(2,1)S(1)}, u32[]{:S(2)}, u32[]{:S(2)}) %all-to-all-start.1) | async-done | bytes 786464 | tf_op jit(solution)/shard_map/all_to_all | solution.py:150
  123.7 3.9 gather_fusion.1
  130.6 31.7 %all-gather.5.cloned.1.call-done = bf16[4096,256]{1,0:T(8,128)(2,1)} async-done(((bf16[1024,256]{1,0:T(8,128)(2,1)}), bf16[4096,256]{1,0:T(8,128)(2,1)}) %all-gather.5.cloned.1.call-update) | async-done | bytes 2097168 | tf_op jit(solution)/shard_map/all_gather | solution.py:13
  168.0 35.8 %while.39 = (s32[]{:T(128)}, f32[64,256]{1,0:T(8,128)S(1)}, f32[256]{0:T(256)S(1)}, f32[256,32]{0,1:T(8,128)S(1)}, bf16[2,512,256]{2,1,0:T(8,128)(2,1)S(1)}, /*i...) while((s32[]{:T(128)}, f32[64,256]{1,0:T(8,128)S(1)}, ...), condition=%wide.region_11.12_spmd.clone, body=%wide.region_9.11_spmd.clone.sunk | while | flops 556843264 | bytes 33839300 | solution.py:90
  173.9 4.0 fusion.134
  178.4 3.4 fusion.136
  191.8 4.0 fusion.134
  196.3 3.4 fusion.136
  203.8 5.4 %gather_fusion.3 = bf16[1536,256]{1,0:T(8,128)(2,1)} fusion(bf16[1024,256]{1,0:T(8,128)(2,1)S(1)} %bitcast.187, s32[2048]{0:T(1024)S(1)} %pad_clamp_fusion), kind=kCustom, calls=%fused_computation.3 | custom fusion | bytes 1579008 | tf_op jit(solution)/shard_map/gather | solution.py:149
  209.2 10.6 %all-to-all-start.2 = ((bf16[64,24,256]{2,1,0:T(8,128)(2,1)}), bf16[64,24,256]{2,1,0:T(8,128)(2,1)S(1)}, u32[]{:S(2)}, u32[]{:S(2)}) async-start(bf16[64,24,256]{2,1,0:T(8,128)(2,1)} %bitcast.28), calls=%async_computation.2 | async-start | bytes 1572864 | tf_op jit(solution)/shard_map/all_to_all | solution.py:150
  220.0 5.7 %gather_fusion.7 = bf16[1024,256]{1,0:T(8,128)(2,1)} fusion(bf16[1024,256]{1,0:T(8,128)(2,1)} %param.19, s32[1024]{0:T(1024)S(1)} %fusion.78), kind=kCustom, calls=%fused_computation.7 | custom fusion | bytes 1052672 | tf_op jit(solution)/shard_map/gather | solution.py:157
  225.7 4.6 gather_fusion.6
  230.5 4.5 gather_fusion.5
  238.0 3.6 all-to-all-done.2
  241.6 4.9 %gather_fusion.4 = bf16[1024,256]{1,0:T(8,128)(2,1)} fusion(bf16[1536,256]{1,0:T(8,128)(2,1)S(1)} %bitcast.200, s32[1024]{0:T(1024)S(1)} %broadcast_clamp_fusion), kind=kCustom, calls=%fused_computation.4 | custom fusion | bytes 1052672 | tf_op jit(solution)/shard_map/gather | solution.py:151
  246.6 3.1 fusion.28
  254.5 3.1 fusion.43
  257.6 105.9 %psum.30 = f32[2,256]{1,0:T(2,128)S(1)} all-reduce(f32[2,256]{1,0:T(2,128)S(1)} %pad_maximum_fusion.8), channel_id=1, replica_groups=mesh['ent'=64,'rel'=4] {'ent'}, use_global_device_ids=true, to_apply=%region_16.17 | all-reduce | flops 512 | bytes 4096 | tf_op jit(solution)/shard_map/psum | solution.py:165
  364.2 71.5 %all-reduce.3.cloned.1.call-done = (f32[328,256]{1,0:T(8,128)}, f32[2,64,256]{2,1,0:T(8,128)}, f32[2,256,32]{1,2,0:T(8,128)}) async-done(((f32[328,256]{1,0:T(8,128)}, f32[2,64,256]{2,1,0:T(8,128)}, f32[2,256,32]{1,2,0:T(8,128)}), (f32[328,256]{1,0:T(8,128)}, f32[2,64,256]{2,1,0:T(8,128)}, f32[2,256,32]{1,2,0:T(8,128)})) %all-reduce.3.cloned.1.call-update) | async-done | bytes 532496 | tf_op jit(solution)/shard_map/psum | solution.py:165
  440.4 28.1 %all-gather.7.cloned.1.call-done = bf16[4096,256]{1,0:T(8,128)(2,1)} async-done(((bf16[1024,256]{1,0:T(8,128)(2,1)}), bf16[4096,256]{1,0:T(8,128)(2,1)}) %all-gather.7.cloned.1.call-update) | async-done | bytes 2097168 | tf_op jit(solution)/shard_map/all_gather | solution.py:13
  (172 shorter events, 76.4 us)
Async XLA Ops:
  7.2 102.1 %copy-start = (bf16[328,256]{1,0:T(8,128)(2,1)S(1)}, bf16[328,256]{1,0:T(8,128)(2,1)}, u32[]{:S(2)}) copy-start(bf16[328,256]{1,0:T(8,128)(2,1)} %param.24) | copy-start | bytes 503812
  33.1 52.7 %all-to-all-start = ((s32[64,1,24]{2,1,0:T(1,128)}), s32[64,1,24]{2,1,0:T(1,128)S(1)}, u32[]{:S(2)}, u32[]{:S(2)}) async-start(s32[64,1,24]{2,1,0:T(1,128)} %bitcast.13), calls=%async_computation | async-start | bytes 65536 | tf_op jit(solution)/shard_map/all_to_all | solution.py:132
  64.4 1.0 copy-start.1
  82.5 1.0 copy-start.1
  85.9 5.5 %copy-start.11 = (f32[256,32]{0,1:T(8,128)}, f32[256,32]{0,1:T(8,128)S(1)}, u32[]{:S(2)}) copy-start(f32[256,32]{0,1:T(8,128)S(1)} %get-tuple-element.146) | copy-start | bytes 98308
  86.0 16.1 %copy-start.19 = (s32[2,1]{0,1:T(1,128)S(1)}, s32[2,1]{0,1:T(1,128)}, u32[]{:S(2)}) copy-start(s32[2,1]{0,1:T(1,128)} %param.29) | copy-start | bytes 28
  86.0 18.0 %copy-start.20 = (s32[2,2]{1,0:T(2,128)S(1)}, s32[2,2]{1,0:T(2,128)}, u32[]{:S(2)}) copy-start(s32[2,2]{1,0:T(2,128)} %param.28) | copy-start | bytes 52
  86.0 18.7 %copy-start.15 = (s32[1024]{0:T(1024)S(1)}, s32[1024]{0:T(1024)}, u32[]{:S(2)}) copy-start(s32[1024]{0:T(1024)} %param.30) | copy-start | bytes 12292
  91.4 17.9 %copy-start.13 = (s32[1024]{0:T(1024)S(1)}, s32[1024]{0:T(1024)}, u32[]{:S(2)}) copy-start(s32[1024]{0:T(1024)} %param.31) | copy-start | bytes 12292
  91.4 32.3 %all-to-all-start.1 = ((bf16[64,24,256]{2,1,0:T(8,128)(2,1)}), bf16[64,24,256]{2,1,0:T(8,128)(2,1)S(1)}, u32[]{:S(2)}, u32[]{:S(2)}) async-start(bf16[64,24,256]{2,1,0:T(8,128)(2,1)} %bitcast.15), calls=%async_computation.1 | async-start | bytes 1572864 | tf_op jit(solution)/shard_map/all_to_all | solution.py:150
  101.9 60.4 %all-gather.5.cloned.1.call-start = ((), (), s32[]{:S(2)}) async-start(), calls=%async_computation.3 | async-start | bytes 2621440 | tf_op jit(solution)/shard_map/all_gather | solution.py:13
  109.2 19.4 %copy-start.17 = (f32[1024]{0:T(1024)}, f32[1024]{0:T(1024)S(1)}, u32[]{:S(2)}) copy-start(f32[1024]{0:T(1024)S(1)} %gather_fusion.2) | copy-start | bytes 12292
  109.8 18.9 %copy-start.5 = (f32[1024,256]{1,0:T(8,128)}, f32[1024,256]{1,0:T(8,128)S(1)}, u32[]{:S(2)}) copy-start(f32[1024,256]{1,0:T(8,128)S(1)} %fusion.40) | copy-start | bytes 3145732
  127.7 2.8 copy-start.7
  128.7 35.7 %copy-start.4 = (f32[2,512,256]{2,1,0:T(8,128)S(1)}, f32[2,512,256]{2,1,0:T(8,128)}, u32[]{:S(2)}) copy-start(f32[2,512,256]{2,1,0:T(8,128)} %get-tuple-element.137) | copy-start | bytes 3145732
  165.7 1.2 copy-start.3
  182.6 1.0 copy-start.2
  200.5 1.0 copy-start.2
  209.2 32.5 %all-to-all-start.2 = ((bf16[64,24,256]{2,1,0:T(8,128)(2,1)}), bf16[64,24,256]{2,1,0:T(8,128)(2,1)S(1)}, u32[]{:S(2)}, u32[]{:S(2)}) async-start(bf16[64,24,256]{2,1,0:T(8,128)(2,1)} %bitcast.28), calls=%async_computation.2 | async-start | bytes 1572864 | tf_op jit(solution)/shard_map/all_to_all | solution.py:150
  219.8 10.6 %copy-start.21 = (pred[8]{0:T(512)(128)(4,1)S(1)}, pred[8]{0:T(512)(128)(4,1)}, u32[]{:S(2)}) copy-start(pred[8]{0:T(512)(128)(4,1)} %get-tuple-element.390) | copy-start | bytes 28
  219.8 215.9 %all-reduce.3.cloned.1.call-start = ((), (), s32[]{:S(2)}) async-start(), calls=%async_computation.5 | async-start | bytes 1064960 | tf_op jit(solution)/shard_map/psum | solution.py:165
  225.7 9.3 %copy-start.8 = (bf16[1024,256]{1,0:T(8,128)(2,1)S(1)}, bf16[1024,256]{1,0:T(8,128)(2,1)}, u32[]{:S(2)}) copy-start(bf16[1024,256]{1,0:T(8,128)(2,1)} %copy-done.7) | copy-start | bytes 1572868
  225.7 9.3 %copy-start.14 = (s32[1024]{0:T(1024)S(1)}, s32[1024]{0:T(1024)}, u32[]{:S(2)}) copy-start(s32[1024]{0:T(1024)} %param.31) | copy-start | bytes 12292
  225.7 9.3 %copy-start.18 = (f32[1024]{0:T(1024)S(1)}, f32[1024]{0:T(1024)}, u32[]{:S(2)}) copy-start(f32[1024]{0:T(1024)} %copy-done.17) | copy-start | bytes 12292
  230.4 6.4 %copy-start.12 = (f32[256,32]{0,1:T(8,128)S(1)}, f32[256,32]{0,1:T(8,128)}, u32[]{:S(2)}) copy-start(f32[256,32]{0,1:T(8,128)} %copy-done.11) | copy-start | bytes 98308
  235.0 11.6 %copy-start.6 = (f32[1024,256]{1,0:T(8,128)S(1)}, f32[1024,256]{1,0:T(8,128)}, u32[]{:S(2)}) copy-start(f32[1024,256]{1,0:T(8,128)} %copy-done.5) | copy-start | bytes 3145732
  235.0 11.5 %copy-start.16 = (s32[1024]{0:T(1024)S(1)}, s32[1024]{0:T(1024)}, u32[]{:S(2)}) copy-start(s32[1024]{0:T(1024)} %param.30) | copy-start | bytes 12292
  246.6 5.3 %copy-start.9 = (bf16[1024,256]{1,0:T(8,128)(2,1)S(1)}, bf16[1024,256]{1,0:T(8,128)(2,1)}, u32[]{:S(2)}) copy-start(bf16[1024,256]{1,0:T(8,128)(2,1)} %gather_fusion.4) | copy-start | bytes 1572868
  246.6 5.3 %copy-start.10 = (bf16[1024,256]{1,0:T(8,128)(2,1)S(1)}, bf16[1024,256]{1,0:T(8,128)(2,1)}, u32[]{:S(2)}) copy-start(bf16[1024,256]{1,0:T(8,128)(2,1)} %gather_fusion.7) | copy-start | bytes 1572868
  246.6 6.2 %copy-start.22 = (f32[328,256]{1,0:T(8,128)S(1)}, f32[328,256]{1,0:T(8,128)}, u32[]{:S(2)}) copy-start(f32[328,256]{1,0:T(8,128)} %fusion.38) | copy-start | bytes 1007620
  254.5 214.0 %all-gather.7.cloned.1.call-start = ((), (), s32[]{:S(2)}) async-start(), calls=%async_computation.4 | async-start | bytes 2621440 | tf_op jit(solution)/shard_map/all_gather | solution.py:13
Sparse Core Ops, SparseCore 0:
  130.6 31.5 all-gather.4
  254.6 180.9 all-reduce.2
  437.5 31.0 all-gather.6
